TPU v7x, 512 devices: a whole 4x8x8 slice. The times are simulated.
512 devices in a mesh: wide: 128 (over y, z, core), rep: 4 (over x).
Axes of the slice: x: 4, y: 8, z: 8, core: 2. Of those that a mesh axis runs over, the one named last changes fastest.
Arguments:
- node_feats: bfloat16 [131072, 512], P('wide'), may hold values from -6 to 6
- w_self: bfloat16 [512, 512], replicated, may hold values from -0.25 to 0.25
- w_neigh: bfloat16 [512, 512], replicated, may hold values from -0.25 to 0.25
- send_rows: int32 [128, 128, 32], P('wide', None, 'rep'), may hold values from 0 to 1023
- tile_dst: int32 [128, 4, 128], P('wide', 'rep'), may hold values from 0 to 15
- tile_src: int32 [128, 4, 128], P('wide', 'rep'), may hold values from 0 to 31
- tile_bits: int32 [128, 4, 32768], P('wide', 'rep'), may hold values from 0 to 65280
- norm_count: int32 [131072], P('wide'), may hold values from 512 to 2048
- grad_out: bfloat16 [131072, 512], P(('wide', 'rep')), may hold values from -6 to 6
Outputs:
- out_feats: bfloat16 [131072, 512], P(('wide', 'rep'))
- grad_feats: bfloat16 [131072, 512], P(('wide', 'rep'))
- grad_self: bfloat16 [512, 512], replicated
- grad_neigh: bfloat16 [512, 512], replicated
All inputs are finite; a program needn't handle non-finite values.
Results may differ from a plain program's by a relative error of at most 0.014.
Values may be sent and summed in bfloat16 or wider, within the bound.
No kernel may reach another device: no remote copies, remote signals or barrier semaphores. Data moves between devices by JAX's collectives and lax.ppermute only.
A program may use at most 64 MiB of HBM per device.

v0:
```python
import math
import jax
import jax.numpy as jnp
from jax import lax
from jax.sharding import PartitionSpec as P

BLOCK = 64


def unpack_bits(packed, tile_count, block_size):
    shaped = packed.reshape(tile_count, block_size, block_size // 16)
    shift_list = jnp.arange(16, dtype=jnp.int32)
    bit_grid = jnp.bitwise_and(jnp.right_shift(shaped[..., None], shift_list), 1)
    return bit_grid.reshape(tile_count, block_size, block_size)


def times_transposed(left, right):
    return lax.dot_general(
        left, right, (((1,), (1,)), ((), ())), preferred_element_type=jnp.float32
    )


def on_device(
    node_feats, w_self, w_neigh, send_rows, tile_dst, tile_src, tile_bits, norm_count, grad_out
):
    node_rows, feat_width = node_feats.shape
    peer_count = lax.axis_size("wide")
    replicas = lax.axis_size("rep")
    slot_count = send_rows.shape[2]
    tile_total = tile_dst.shape[2]
    block_size = BLOCK
    quarter = node_rows // replicas
    rep_index = lax.axis_index("rep")
    dst_count = node_rows // block_size
    group_size = math.gcd(tile_total, 32)
    send_index = send_rows[0]
    outgoing = jnp.take(node_feats, send_index.reshape(-1), axis=0).reshape(
        peer_count, slot_count, feat_width
    )
    incoming = lax.all_to_all(outgoing, "wide", split_axis=0, concat_axis=0, tiled=True)
    src_table = jnp.concatenate(
        [node_feats, incoming.reshape(peer_count * slot_count, feat_width)], axis=0
    )
    source_blocks = src_table.reshape(-1, block_size, feat_width)
    src_count = source_blocks.shape[0]
    tile_masks = unpack_bits(tile_bits[0, 0], tile_total, block_size).astype(jnp.bfloat16)
    grouped_masks = tile_masks.reshape(-1, group_size, block_size, block_size)
    grouped_dst = tile_dst[0, 0].reshape(-1, group_size)
    grouped_src = tile_src[0, 0].reshape(-1, group_size)

    def forward_group(running, group_items):
        mask_part, dst_part, src_part = group_items
        picked = jnp.take(source_blocks, src_part, axis=0)
        products = jnp.einsum("tij,tjf->tif", mask_part, picked, preferred_element_type=jnp.float32)
        return (running.at[dst_part].add(products), None)

    partial_sum, _ = lax.scan(
        forward_group,
        jnp.zeros((dst_count, block_size, feat_width), jnp.float32),
        (grouped_masks, grouped_dst, grouped_src),
    )
    partial_sum = partial_sum.reshape(node_rows, feat_width)
    summed = lax.psum(partial_sum, "rep")
    own_sums = lax.dynamic_slice_in_dim(summed, rep_index * quarter, quarter, 0)
    scale_all = lax.rsqrt(norm_count.astype(jnp.float32))
    own_scale = lax.dynamic_slice_in_dim(scale_all, rep_index * quarter, quarter, 0)
    own_feats = lax.dynamic_slice_in_dim(node_feats, rep_index * quarter, quarter, 0)
    own_agg = (own_sums * own_scale[:, None]).astype(jnp.bfloat16)
    pre_act = jnp.dot(own_feats, w_self, preferred_element_type=jnp.float32) + jnp.dot(
        own_agg, w_neigh, preferred_element_type=jnp.float32
    )
    sigmoid = jax.nn.sigmoid(pre_act)
    out_feats = (pre_act * sigmoid).astype(jnp.bfloat16)
    grad_pre = (grad_out.astype(jnp.float32) * sigmoid * (1.0 + pre_act * (1.0 - sigmoid))).astype(
        jnp.bfloat16
    )
    dims_rows = (((0,), (0,)), ((), ()))
    self_term = lax.dot_general(own_feats, grad_pre, dims_rows, preferred_element_type=jnp.float32)
    neigh_term = lax.dot_general(own_agg, grad_pre, dims_rows, preferred_element_type=jnp.float32)
    summed_self, summed_neigh = lax.psum((self_term, neigh_term), ("wide", "rep"))
    own_grad_agg = (times_transposed(grad_pre, w_neigh) * own_scale[:, None]).astype(jnp.bfloat16)
    grad_agg = lax.all_gather(own_grad_agg, "rep", axis=0, tiled=True)
    agg_blocks = grad_agg.reshape(dst_count, block_size, feat_width)

    def backward_group(running, group_items):
        mask_part, dst_part, src_part = group_items
        picked = jnp.take(agg_blocks, dst_part, axis=0)
        products = jnp.einsum("tij,tif->tjf", mask_part, picked, preferred_element_type=jnp.float32)
        return (running.at[src_part].add(products), None)

    table_grad, _ = lax.scan(
        backward_group,
        jnp.zeros((src_count, block_size, feat_width), jnp.float32),
        (grouped_masks, grouped_dst, grouped_src),
    )
    table_grad = table_grad.reshape(src_count * block_size, feat_width)
    local_grad = table_grad[:node_rows]
    halo_grad = (
        table_grad[node_rows:].astype(jnp.bfloat16).reshape(peer_count, slot_count, feat_width)
    )
    returned = lax.all_to_all(halo_grad, "wide", split_axis=0, concat_axis=0, tiled=True)
    returned_rows = (
        jnp.zeros((node_rows, feat_width), jnp.float32)
        .at[send_index.reshape(-1)]
        .add(returned.reshape(-1, feat_width).astype(jnp.float32))
    )
    own_total = lax.psum_scatter(
        (local_grad + returned_rows).astype(jnp.bfloat16), "rep", scatter_dimension=0, tiled=True
    ).astype(jnp.float32)
    grad_feats = (own_total + times_transposed(grad_pre, w_self)).astype(jnp.bfloat16)
    return (
        out_feats,
        grad_feats,
        summed_self.astype(jnp.bfloat16),
        summed_neigh.astype(jnp.bfloat16),
    )


def solution(mesh):
    in_specs = (
        P("wide", None),
        P(),
        P(),
        P("wide", None, "rep"),
        P("wide", "rep", None),
        P("wide", "rep", None),
        P("wide", "rep", None),
        P("wide"),
        P(("wide", "rep"), None),
    )
    out_specs = (P(("wide", "rep"), None), P(("wide", "rep"), None), P(), P())
    return jax.shard_map(
        on_device, mesh=mesh, in_specs=in_specs, out_specs=out_specs, check_vma=False
    )
```

profile of v0, /device:TPU:1, one launch (start us, length us, event | category | flops | bytes accessed | tf_op | source)
XLA Modules:
  0.0 459.9 jit_solution(16109861953868291241)
XLA Ops:
  9.0 5.4 %gather_fusion.2 = bf16[1024,512]{1,0:T(8,128)(2,1)S(1)} fusion(bf16[1024,512]{1,0:T(8,128)(2,1)} %param.13, s32[1024]{0:T(1024)S(1)} %broadcast_clamp_fusion), kind=kCustom, calls=%fused_computation.2 | custom fusion | bytes 2101248 | tf_op jit(solution)/shard_map/jit(_take)/gather | solution.py:37
  15.5 18.4 %all-to-all-start = ((bf16[128,8,512]{2,1,0:T(8,128)(2,1)}), bf16[128,8,512]{2,1,0:T(8,128)(2,1)S(1)}, u32[]{:S(2)}, u32[]{:S(2)}) async-start(bf16[128,8,512]{2,1,0:T(8,128)(2,1)} %bitcast_select_fusion), calls=%async_computation | async-start | bytes 2097152 | tf_op jit(solution)/shard_map/all_to_all | solution.py:40
  37.1 5.7 %shift_right_arithmetic.23 = s32[128,64,4]{2,1,0:T(8,128)} reshape(s32[32768]{0:T(1024)S(1)} %reduce.10) | data formatting | bytes 262144 | tf_op jit(solution)/shard_map/shift_right_arithmetic | solution.py:13
  48.2 16.2 %all-to-all-done = bf16[128,8,512]{2,1,0:T(8,128)(2,1)S(1)} async-done(((bf16[128,8,512]{2,1,0:T(8,128)(2,1)}), bf16[128,8,512]{2,1,0:T(8,128)(2,1)S(1)}, u32[]{:S(2)}, u32[]{:S(2)}) %all-to-all-start) | async-done | bytes 1048608 | tf_op jit(solution)/shard_map/all_to_all | solution.py:40
  66.1 58.5 %while.20 = (s32[]{:T(128)}, f32[16,64,512]{2,1,0:T(8,128)S(1)}, s32[4,32]{1,0:T(4,128)S(1)}, bf16[4,32,64,64]{2,3,1,0:T(8,128)(2,1)}, s32[4,32]{1,0:T(4,128)S(1)}, /*index=5*/bf16[32,64,512]{2,1,0:T(8,128)(2,1)}, s32[]{:T(128)}) while((s32[]{:T(128)}, f32[16,64,512]{2,1,0:T(8,128)S(1)}, s32[4,32]{1,0:T(4,128)S(1)}, ...), condition=%wide.region_2.3_spmd, body=%wide.region_0.0_spmd.sunk | while | flops 136316288 | bytes 23598240 | solution.py:57
  69.8 4.5 fusion.53
  74.3 6.5 %scatter_fusion = f32[16,64,512]{2,1,0:T(8,128)S(1)} fusion(f32[16,64,512]{2,1,0:T(8,128)S(1)} %get-tuple-element.204, s32[32]{0:T(128)S(1)} %get-tuple-element.186, f32[32,64,512]{2,1,0:T(8,128)} %fusion.53), kind=kCustom, calls=%fused_computation.3.clone.1 | custom fusion | flops 1048576 | bytes 12583040 | tf_op jit(solution)/shard_map/while/body/eval_jaxpr/scatter-add | solution.py:55
  84.4 4.5 fusion.53
  88.9 6.5 %scatter_fusion = f32[16,64,512]{2,1,0:T(8,128)S(1)} fusion(f32[16,64,512]{2,1,0:T(8,128)S(1)} %get-tuple-element.204, s32[32]{0:T(128)S(1)} %get-tuple-element.186, f32[32,64,512]{2,1,0:T(8,128)} %fusion.53), kind=kCustom, calls=%fused_computation.3.clone.1 | custom fusion | flops 1048576 | bytes 12583040 | tf_op jit(solution)/shard_map/while/body/eval_jaxpr/scatter-add | solution.py:55
  99.1 4.5 fusion.53
  103.5 6.5 %scatter_fusion = f32[16,64,512]{2,1,0:T(8,128)S(1)} fusion(f32[16,64,512]{2,1,0:T(8,128)S(1)} %get-tuple-element.204, s32[32]{0:T(128)S(1)} %get-tuple-element.186, f32[32,64,512]{2,1,0:T(8,128)} %fusion.53), kind=kCustom, calls=%fused_computation.3.clone.1 | custom fusion | flops 1048576 | bytes 12583040 | tf_op jit(solution)/shard_map/while/body/eval_jaxpr/scatter-add | solution.py:55
  113.7 4.5 fusion.53
  118.2 6.5 %scatter_fusion = f32[16,64,512]{2,1,0:T(8,128)S(1)} fusion(f32[16,64,512]{2,1,0:T(8,128)S(1)} %get-tuple-element.204, s32[32]{0:T(128)S(1)} %get-tuple-element.186, f32[32,64,512]{2,1,0:T(8,128)} %fusion.53), kind=kCustom, calls=%fused_computation.3.clone.1 | custom fusion | flops 1048576 | bytes 12583040 | tf_op jit(solution)/shard_map/while/body/eval_jaxpr/scatter-add | solution.py:55
  127.6 62.0 %all-reduce.4.cloned.1.call-done = f32[1024,512]{1,0:T(8,128)} async-done(((f32[1024,512]{1,0:T(8,128)}), f32[1024,512]{1,0:T(8,128)}) %all-reduce.4.cloned.1.call-update) | async-done | bytes 2097168 | tf_op jit(solution)/shard_map/psum | solution.py:63
  193.0 28.4 %all-gather.2.cloned.1.call-done = bf16[1024,512]{1,0:T(8,128)(2,1)} async-done(((bf16[256,512]{1,0:T(8,128)(2,1)}), bf16[1024,512]{1,0:T(8,128)(2,1)}) %all-gather.2.cloned.1.call-update) | async-done | bytes 1048592 | tf_op jit(solution)/shard_map/all_gather | solution.py:82
  223.9 62.5 %while.21 = (s32[]{:T(128)}, f32[32,64,512]{2,1,0:T(8,128)}, s32[4,32]{1,0:T(4,128)S(1)}, bf16[4,32,64,64]{2,3,1,0:T(8,128)(2,1)}, s32[4,32]{1,0:T(4,128)S(1)}, /*index=5*/bf16[16,64,512]{2,1,0:T(8,128)(2,1)}, s32[]{:T(128)}) while((s32[]{:T(128)}, f32[32,64,512]{2,1,0:T(8,128)}, s32[4,32]{1,0:T(4,128)S(1)}, ...), condition=%wide.region_6.7_spmd, body=%wide.region_4.6_spmd.sunk | while | flops 136316288 | bytes 23598240 | solution.py:91
  229.7 9.8 %scatter_fusion.1 = f32[32,64,512]{2,1,0:T(8,128)} fusion(f32[32,64,512]{2,1,0:T(8,128)} %get-tuple-element.225, s32[32]{0:T(128)S(1)} %get-tuple-element.194, f32[32,64,512]{2,1,0:T(8,128)} %fusion.57), kind=kCustom, calls=%fused_computation.4.clone.1 | custom fusion | flops 1048576 | bytes 12583040 | tf_op jit(solution)/shard_map/while/body/eval_jaxpr/scatter-add | solution.py:89
  245.1 9.8 %scatter_fusion.1 = f32[32,64,512]{2,1,0:T(8,128)} fusion(f32[32,64,512]{2,1,0:T(8,128)} %get-tuple-element.225, s32[32]{0:T(128)S(1)} %get-tuple-element.194, f32[32,64,512]{2,1,0:T(8,128)} %fusion.57), kind=kCustom, calls=%fused_computation.4.clone.1 | custom fusion | flops 1048576 | bytes 12583040 | tf_op jit(solution)/shard_map/while/body/eval_jaxpr/scatter-add | solution.py:89
  260.6 10.0 %scatter_fusion.1 = f32[32,64,512]{2,1,0:T(8,128)} fusion(f32[32,64,512]{2,1,0:T(8,128)} %get-tuple-element.225, s32[32]{0:T(128)S(1)} %get-tuple-element.194, f32[32,64,512]{2,1,0:T(8,128)} %fusion.57), kind=kCustom, calls=%fused_computation.4.clone.1 | custom fusion | flops 1048576 | bytes 12583040 | tf_op jit(solution)/shard_map/while/body/eval_jaxpr/scatter-add | solution.py:89
  276.3 10.1 %scatter_fusion.1 = f32[32,64,512]{2,1,0:T(8,128)} fusion(f32[32,64,512]{2,1,0:T(8,128)} %get-tuple-element.225, s32[32]{0:T(128)S(1)} %get-tuple-element.194, f32[32,64,512]{2,1,0:T(8,128)} %fusion.57), kind=kCustom, calls=%fused_computation.4.clone.1 | custom fusion | flops 1048576 | bytes 12583040 | tf_op jit(solution)/shard_map/while/body/eval_jaxpr/scatter-add | solution.py:89
  289.2 15.9 %all-to-all-start.1 = ((bf16[128,8,512]{2,1,0:T(8,128)(2,1)}), bf16[128,8,512]{2,1,0:T(8,128)(2,1)}, u32[]{:S(2)}, u32[]{:S(2)}) async-start(bf16[128,8,512]{2,1,0:T(8,128)(2,1)} %bitcast.21), calls=%async_computation.1 | async-start | bytes 2097152 | tf_op jit(solution)/shard_map/all_to_all | solution.py:101
  307.0 28.2 %all-to-all-done.1 = bf16[128,8,512]{2,1,0:T(8,128)(2,1)} async-done(((bf16[128,8,512]{2,1,0:T(8,128)(2,1)}), bf16[128,8,512]{2,1,0:T(8,128)(2,1)}, u32[]{:S(2)}, u32[]{:S(2)}) %all-to-all-start.1) | async-done | bytes 1048608 | tf_op jit(solution)/shard_map/all_to_all | solution.py:101
  335.2 8.0 %scatter_custom_fusion.2 = f32[1024,512]{1,0:T(8,128)S(1)} fusion(f32[1024,512]{1,0:T(8,128)S(1)} %bitcast.83, s32[1024]{0:T(1024)S(1)} %bitcast.86, bf16[128,8,512]{2,1,0:T(8,128)(2,1)} %all-to-all-done.1), kind=kCustom, calls=%fused_computation.45 | custom fusion | flops 1048576 | bytes 3145728 | tf_op jit(solution)/shard_map/scatter-add | solution.py:105
  347.0 104.4 %all-reduce.5 = (bf16[512,512]{1,0:T(8,128)(2,1)}, bf16[512,512]{1,0:T(8,128)(2,1)}) all-reduce(f32[512,512]{1,0:T(8,128)S(1)} %fusion.27, f32[512,512]{1,0:T(8,128)S(1)} %fusion.33), channel_id=1, replica_groups=mesh['wide'=128,'rep'=4] {'wide','rep'}, use_global_device_ids=true, to_apply=%region_9.10 | all-reduce | flops 524288 | bytes 3145728 | tf_op jit(solution)/shard_map/psum | solution.py:80
  (91 shorter events, 69.8 us)
Async XLA Ops:
  7.2 182.5 %copy-start = (bf16[512,512]{1,0:T(8,128)(2,1)S(1)}, bf16[512,512]{1,0:T(8,128)(2,1)}, u32[]{:S(2)}) copy-start(bf16[512,512]{1,0:T(8,128)(2,1)} %param.15) | copy-start | bytes 1572868
  14.3 20.2 %copy-start.6 = (s32[1,1,128]{2,1,0:T(1,128)S(1)}, s32[1,1,128]{2,1,0:T(1,128)}, u32[]{:S(2)}) copy-start(s32[1,1,128]{2,1,0:T(1,128)} %param.17) | copy-start | bytes 1540
  14.3 20.9 %copy-start.7 = (s32[1,1,128]{2,1,0:T(1,128)S(1)}, s32[1,1,128]{2,1,0:T(1,128)}, u32[]{:S(2)}) copy-start(s32[1,1,128]{2,1,0:T(1,128)} %param.18) | copy-start | bytes 1540
  14.4 21.8 %copy-start.4 = (s32[1,1,32768]{2,1,0:T(1,128)S(1)}, s32[1,1,32768]{2,1,0:T(1,128)}, u32[]{:S(2)}) copy-start(s32[1,1,32768]{2,1,0:T(1,128)} %param.19) | copy-start | bytes 393220
  15.5 48.9 %all-to-all-start = ((bf16[128,8,512]{2,1,0:T(8,128)(2,1)}), bf16[128,8,512]{2,1,0:T(8,128)(2,1)S(1)}, u32[]{:S(2)}, u32[]{:S(2)}) async-start(bf16[128,8,512]{2,1,0:T(8,128)(2,1)} %bitcast_select_fusion), calls=%async_computation | async-start | bytes 2097152 | tf_op jit(solution)/shard_map/all_to_all | solution.py:40
  34.0 155.7 %all-reduce.4.cloned.1.call-start = ((), (), s32[]{:S(2)}) async-start(), calls=%async_computation.3 | async-start | bytes 4194304 | tf_op jit(solution)/shard_map/psum | solution.py:63
  46.1 18.3 %copy-start.2 = (bf16[1024,512]{1,0:T(8,128)(2,1)S(1)}, bf16[1024,512]{1,0:T(8,128)(2,1)}, u32[]{:S(2)}) copy-start(bf16[1024,512]{1,0:T(8,128)(2,1)} %param.13) | copy-start | bytes 3145732
  124.7 1.3 copy-start.1
  124.7 1.6 copy-start.5
  124.7 1.7 copy-start.3
  126.0 95.4 %all-gather.2.cloned.1.call-start = ((), (), s32[]{:S(2)}) async-start(), calls=%async_computation.4 | async-start | bytes 1310720 | tf_op jit(solution)/shard_map/all_gather | solution.py:82
  289.2 46.0 %all-to-all-start.1 = ((bf16[128,8,512]{2,1,0:T(8,128)(2,1)}), bf16[128,8,512]{2,1,0:T(8,128)(2,1)}, u32[]{:S(2)}, u32[]{:S(2)}) async-start(bf16[128,8,512]{2,1,0:T(8,128)(2,1)} %bitcast.21), calls=%async_computation.1 | async-start | bytes 2097152 | tf_op jit(solution)/shard_map/all_to_all | solution.py:101
  305.1 146.3 %reduce-scatter.2.cloned.1.call-start = ((), (), s32[]{:S(2)}) async-start(), calls=%async_computation.5 | async-start | bytes 1310720 | tf_op jit(solution)/shard_map/reduce_scatter | solution.py:107
Sparse Core Ops, SparseCore 0:
  126.2 63.4 all-reduce.3
  193.2 28.2 all-gather.1
  344.4 20.2 reduce-scatter.1
where the time goes:
time: 462 us; the launch traced here: 460 us
  waiting for transfers between devices  135 us (29%)
  blocking collectives  104 us (23%)
  other arithmetic  82.7 us (18%)
  local copies, waits for them, and re-layouts  47 us (10%)
  matrix products  42.2 us (9%)
  starting transfers between devices  34.6 us (7%)
  between operations  14 us (3%)
    psum x1, blocking collectives, on_device(): lax.psum((self_term, neigh_term), ('wide', 'rep'))  104 us
    psum x1, waiting for transfers between devices, on_device(): summed = lax.psum(partial_sum, 'rep')  62 us
    scatter-add x4, other arithmetic, backward_group(): return (running.at[src_part].add(products), None)  39.6 us
    all_gather x1, waiting for transfers between devices, on_device(): grad_agg = lax.all_gather(own_grad_agg, 'rep', axis=0, tiled=True)  28.4 us
    all_to_all x1, waiting for transfers between devices, on_device(): lax.all_to_all(halo_grad, 'wide', split_axis=0, concat_axis=0, tiled=True)  28.2 us
    scatter-add x4, other arithmetic, forward_group(): return (running.at[dst_part].add(products), None)  25.9 us
    all_to_all x1, starting transfers between devices, on_device(): lax.all_to_all(outgoing, 'wide', split_axis=0, concat_axis=0, tiled=True)  18.4 us
    dot_general x4, matrix products, forward_group(): jnp.einsum('tij,tjf->tif', mask_part, picked, preferred_element_type=jnp....  17.9 us
  transfers between devices with their start and end apart: 5, of which 4 were waited for; matrix products, arithmetic and copies ran while one was open for 4% of the time, Pallas kernels for 0%

commit v1 on v0

--- a/solution.py
+++ b/solution.py
@@ -60,7 +60,9 @@
         (grouped_masks, grouped_dst, grouped_src),
     )
     partial_sum = partial_sum.reshape(node_rows, feat_width)
-    summed = lax.psum(partial_sum, "rep")
+    summed = partial_sum
+    for hop in (1, 2):
+        summed = summed + lax.ppermute(summed, "rep", [(dev, dev ^ hop) for dev in range(4)])
     own_sums = lax.dynamic_slice_in_dim(summed, rep_index * quarter, quarter, 0)
     scale_all = lax.rsqrt(norm_count.astype(jnp.float32))
     own_scale = lax.dynamic_slice_in_dim(scale_all, rep_index * quarter, quarter, 0)

time: 462 us -> 495 us (1.071)
  waiting for transfers between devices: 135 us -> 158 us
  starting transfers between devices: 34.6 us -> 42.3 us
    ppermute x0 -> x2, waiting for transfers between devices: none -> 86.9 us  [on_device(): lax.ppermute(summed, 'rep', [(dev, dev ^ hop) for dev in range(4)])]
    psum x1 -> x0, waiting for transfers between devices: 62 us -> none  [on_device(): summed = lax.psum(partial_sum, 'rep')]
    ppermute x0 -> x2, starting transfers between devices: none -> 8 us  [on_device(): lax.ppermute(summed, 'rep', [(dev, dev ^ hop) for dev in range(4)])]
  transfers between devices with their start and end apart: 5 -> 6, of which waited for: 4 -> 5; matrix products, arithmetic and copies ran while one was open for 4% -> 4% of each run, Pallas kernels for 0% -> 0%
where the time goes in v1:
time: 495 us; the launch traced here: 493 us
  waiting for transfers between devices  158 us (32%)
  blocking collectives  105 us (21%)
  other arithmetic  85.6 us (17%)
  local copies, waits for them, and re-layouts  46.4 us (9%)
  starting transfers between devices  42.3 us (9%)
  matrix products  41.8 us (8%)
  between operations  14.3 us (3%)
    psum x1, blocking collectives, on_device(): lax.psum((self_term, neigh_term), ('wide', 'rep'))  105 us
    ppermute x2, waiting for transfers between devices, on_device(): lax.ppermute(summed, 'rep', [(dev, dev ^ hop) for dev in range(4)])  86.9 us
    scatter-add x4, other arithmetic, backward_group(): return (running.at[src_part].add(products), None)  39.6 us
    all_to_all x1, waiting for transfers between devices, on_device(): lax.all_to_all(halo_grad, 'wide', split_axis=0, concat_axis=0, tiled=True)  28.2 us
    all_gather x1, waiting for transfers between devices, on_device(): grad_agg = lax.all_gather(own_grad_agg, 'rep', axis=0, tiled=True)  26.6 us
    scatter-add x4, other arithmetic, forward_group(): return (running.at[dst_part].add(products), None)  25.9 us
    all_to_all x1, starting transfers between devices, on_device(): lax.all_to_all(outgoing, 'wide', split_axis=0, concat_axis=0, tiled=True)  18.4 us
    dot_general x4, matrix products, forward_group(): jnp.einsum('tij,tjf->tif', mask_part, picked, preferred_element_type=jnp....  17.9 us
  transfers between devices with their start and end apart: 6, of which 5 were waited for; matrix products, arithmetic and copies ran while one was open for 4% of the time, Pallas kernels for 0%

profile of v1, /device:TPU:1, one launch (start us, length us, event | category | flops | bytes accessed | tf_op | source)
XLA Modules:
  0.0 493.0 jit_solution(9854447556488763968)
XLA Ops:
  9.0 5.3 %gather_fusion.2 = bf16[1024,512]{1,0:T(8,128)(2,1)S(1)} fusion(bf16[1024,512]{1,0:T(8,128)(2,1)} %param.13, s32[1024]{0:T(1024)S(1)} %broadcast_clamp_fusion), kind=kCustom, calls=%fused_computation.2 | custom fusion | bytes 2101248 | tf_op jit(solution)/shard_map/jit(_take)/gather | solution.py:37
  15.5 18.4 %all-to-all-start = ((bf16[128,8,512]{2,1,0:T(8,128)(2,1)}), bf16[128,8,512]{2,1,0:T(8,128)(2,1)S(1)}, u32[]{:S(2)}, u32[]{:S(2)}) async-start(bf16[128,8,512]{2,1,0:T(8,128)(2,1)} %bitcast_select_fusion), calls=%async_computation | async-start | bytes 2097152 | tf_op jit(solution)/shard_map/all_to_all | solution.py:40
  36.2 5.7 %shift_right_arithmetic.23 = s32[128,64,4]{2,1,0:T(8,128)} reshape(s32[32768]{0:T(1024)S(1)} %reduce.10) | data formatting | bytes 262144 | tf_op jit(solution)/shard_map/shift_right_arithmetic | solution.py:13
  48.3 16.2 %all-to-all-done = bf16[128,8,512]{2,1,0:T(8,128)(2,1)S(1)} async-done(((bf16[128,8,512]{2,1,0:T(8,128)(2,1)}), bf16[128,8,512]{2,1,0:T(8,128)(2,1)S(1)}, u32[]{:S(2)}, u32[]{:S(2)}) %all-to-all-start) | async-done | bytes 1048608 | tf_op jit(solution)/shard_map/all_to_all | solution.py:40
  66.1 58.5 %while.20 = (s32[]{:T(128)}, f32[16,64,512]{2,1,0:T(8,128)S(1)}, s32[4,32]{1,0:T(4,128)S(1)}, bf16[4,32,64,64]{2,3,1,0:T(8,128)(2,1)}, s32[4,32]{1,0:T(4,128)S(1)}, /*index=5*/bf16[32,64,512]{2,1,0:T(8,128)(2,1)}, s32[]{:T(128)}) while((s32[]{:T(128)}, f32[16,64,512]{2,1,0:T(8,128)S(1)}, s32[4,32]{1,0:T(4,128)S(1)}, ...), condition=%wide.region_2.3_spmd, body=%wide.region_0.0_spmd.sunk | while | flops 136316288 | bytes 23598240 | solution.py:57
  74.3 6.5 %scatter_fusion = f32[16,64,512]{2,1,0:T(8,128)S(1)} fusion(f32[16,64,512]{2,1,0:T(8,128)S(1)} %get-tuple-element.204, s32[32]{0:T(128)S(1)} %get-tuple-element.186, f32[32,64,512]{2,1,0:T(8,128)} %fusion.57), kind=kCustom, calls=%fused_computation.3.clone.1 | custom fusion | flops 1048576 | bytes 12583040 | tf_op jit(solution)/shard_map/while/body/eval_jaxpr/scatter-add | solution.py:55
  84.4 4.5 fusion.57
  88.9 6.5 %scatter_fusion = f32[16,64,512]{2,1,0:T(8,128)S(1)} fusion(f32[16,64,512]{2,1,0:T(8,128)S(1)} %get-tuple-element.204, s32[32]{0:T(128)S(1)} %get-tuple-element.186, f32[32,64,512]{2,1,0:T(8,128)} %fusion.57), kind=kCustom, calls=%fused_computation.3.clone.1 | custom fusion | flops 1048576 | bytes 12583040 | tf_op jit(solution)/shard_map/while/body/eval_jaxpr/scatter-add | solution.py:55
  103.5 6.5 %scatter_fusion = f32[16,64,512]{2,1,0:T(8,128)S(1)} fusion(f32[16,64,512]{2,1,0:T(8,128)S(1)} %get-tuple-element.204, s32[32]{0:T(128)S(1)} %get-tuple-element.186, f32[32,64,512]{2,1,0:T(8,128)} %fusion.57), kind=kCustom, calls=%fused_computation.3.clone.1 | custom fusion | flops 1048576 | bytes 12583040 | tf_op jit(solution)/shard_map/while/body/eval_jaxpr/scatter-add | solution.py:55
  113.7 4.5 fusion.57
  118.2 6.5 %scatter_fusion = f32[16,64,512]{2,1,0:T(8,128)S(1)} fusion(f32[16,64,512]{2,1,0:T(8,128)S(1)} %get-tuple-element.204, s32[32]{0:T(128)S(1)} %get-tuple-element.186, f32[32,64,512]{2,1,0:T(8,128)} %fusion.57), kind=kCustom, calls=%fused_computation.3.clone.1 | custom fusion | flops 1048576 | bytes 12583040 | tf_op jit(solution)/shard_map/while/body/eval_jaxpr/scatter-add | solution.py:55
  127.9 44.6 %collective-permute-done = f32[1024,512]{1,0:T(8,128)S(1)} collective-permute-done((f32[1024,512]{1,0:T(8,128)S(1)}, f32[1024,512]{1,0:T(8,128)S(1)}, u32[]{:S(2)}, u32[]{:S(2)}) %collective-permute-start) | collective-permute-done | bytes 2097184 | tf_op jit(solution)/shard_map/ppermute | solution.py:65
  174.3 4.8 collective-permute-start.1
  180.5 42.3 %collective-permute-done.1 = f32[1024,512]{1,0:T(8,128)S(1)} collective-permute-done((f32[1024,512]{1,0:T(8,128)}, f32[1024,512]{1,0:T(8,128)S(1)}, u32[]{:S(2)}, u32[]{:S(2)}) %collective-permute-start.1) | collective-permute-done | bytes 2097184 | tf_op jit(solution)/shard_map/ppermute | solution.py:65
  227.8 26.6 %all-gather.2.cloned.1.call-done = bf16[1024,512]{1,0:T(8,128)(2,1)} async-done(((bf16[256,512]{1,0:T(8,128)(2,1)}), bf16[1024,512]{1,0:T(8,128)(2,1)}) %all-gather.2.cloned.1.call-update) | async-done | bytes 1048592 | tf_op jit(solution)/shard_map/all_gather | solution.py:84
  257.0 62.3 %while.21 = (s32[]{:T(128)}, f32[32,64,512]{2,1,0:T(8,128)}, s32[4,32]{1,0:T(4,128)S(1)}, bf16[4,32,64,64]{2,3,1,0:T(8,128)(2,1)}, s32[4,32]{1,0:T(4,128)S(1)}, /*index=5*/bf16[16,64,512]{2,1,0:T(8,128)(2,1)}, s32[]{:T(128)}) while((s32[]{:T(128)}, f32[32,64,512]{2,1,0:T(8,128)}, s32[4,32]{1,0:T(4,128)S(1)}, ...), condition=%wide.region_5.6_spmd, body=%wide.region_3.5_spmd.sunk | while | flops 136316288 | bytes 23598240 | solution.py:93
  262.7 9.7 %scatter_fusion.1 = f32[32,64,512]{2,1,0:T(8,128)} fusion(f32[32,64,512]{2,1,0:T(8,128)} %get-tuple-element.225, s32[32]{0:T(128)S(1)} %get-tuple-element.194, f32[32,64,512]{2,1,0:T(8,128)} %fusion.61), kind=kCustom, calls=%fused_computation.4.clone.1 | custom fusion | flops 1048576 | bytes 12583040 | tf_op jit(solution)/shard_map/while/body/eval_jaxpr/scatter-add | solution.py:91
  278.1 9.9 %scatter_fusion.1 = f32[32,64,512]{2,1,0:T(8,128)} fusion(f32[32,64,512]{2,1,0:T(8,128)} %get-tuple-element.225, s32[32]{0:T(128)S(1)} %get-tuple-element.194, f32[32,64,512]{2,1,0:T(8,128)} %fusion.61), kind=kCustom, calls=%fused_computation.4.clone.1 | custom fusion | flops 1048576 | bytes 12583040 | tf_op jit(solution)/shard_map/while/body/eval_jaxpr/scatter-add | solution.py:91
  293.7 9.9 %scatter_fusion.1 = f32[32,64,512]{2,1,0:T(8,128)} fusion(f32[32,64,512]{2,1,0:T(8,128)} %get-tuple-element.225, s32[32]{0:T(128)S(1)} %get-tuple-element.194, f32[32,64,512]{2,1,0:T(8,128)} %fusion.61), kind=kCustom, calls=%fused_computation.4.clone.1 | custom fusion | flops 1048576 | bytes 12583040 | tf_op jit(solution)/shard_map/while/body/eval_jaxpr/scatter-add | solution.py:91
  309.3 10.0 %scatter_fusion.1 = f32[32,64,512]{2,1,0:T(8,128)} fusion(f32[32,64,512]{2,1,0:T(8,128)} %get-tuple-element.225, s32[32]{0:T(128)S(1)} %get-tuple-element.194, f32[32,64,512]{2,1,0:T(8,128)} %fusion.61), kind=kCustom, calls=%fused_computation.4.clone.1 | custom fusion | flops 1048576 | bytes 12583040 | tf_op jit(solution)/shard_map/while/body/eval_jaxpr/scatter-add | solution.py:91
  322.1 15.8 %all-to-all-start.1 = ((bf16[128,8,512]{2,1,0:T(8,128)(2,1)}), bf16[128,8,512]{2,1,0:T(8,128)(2,1)}, u32[]{:S(2)}, u32[]{:S(2)}) async-start(bf16[128,8,512]{2,1,0:T(8,128)(2,1)} %bitcast.21), calls=%async_computation.1 | async-start | bytes 2097152 | tf_op jit(solution)/shard_map/all_to_all | solution.py:103
  339.9 28.2 %all-to-all-done.1 = bf16[128,8,512]{2,1,0:T(8,128)(2,1)} async-done(((bf16[128,8,512]{2,1,0:T(8,128)(2,1)}), bf16[128,8,512]{2,1,0:T(8,128)(2,1)}, u32[]{:S(2)}, u32[]{:S(2)}) %all-to-all-start.1) | async-done | bytes 1048608 | tf_op jit(solution)/shard_map/all_to_all | solution.py:103
  368.0 8.0 %scatter_custom_fusion.2 = f32[1024,512]{1,0:T(8,128)S(1)} fusion(f32[1024,512]{1,0:T(8,128)S(1)} %bitcast.86, s32[1024]{0:T(1024)S(1)} %bitcast.89, bf16[128,8,512]{2,1,0:T(8,128)(2,1)} %all-to-all-done.1), kind=kCustom, calls=%fused_computation.45 | custom fusion | flops 1048576 | bytes 3145728 | tf_op jit(solution)/shard_map/scatter-add | solution.py:107
  379.7 104.5 %all-reduce.2 = (bf16[512,512]{1,0:T(8,128)(2,1)}, bf16[512,512]{1,0:T(8,128)(2,1)}) all-reduce(f32[512,512]{1,0:T(8,128)S(1)} %fusion.29, f32[512,512]{1,0:T(8,128)S(1)} %fusion.35), channel_id=1, replica_groups=mesh['wide'=128,'rep'=4] {'wide','rep'}, use_global_device_ids=true, to_apply=%region_8.9 | all-reduce | flops 524288 | bytes 3145728 | tf_op jit(solution)/shard_map/psum | solution.py:82
  (94 shorter events, 83.7 us)
Async XLA Ops:
  7.2 217.5 %copy-start = (bf16[512,512]{1,0:T(8,128)(2,1)S(1)}, bf16[512,512]{1,0:T(8,128)(2,1)}, u32[]{:S(2)}) copy-start(bf16[512,512]{1,0:T(8,128)(2,1)} %param.15) | copy-start | bytes 1572868
  14.3 20.2 %copy-start.6 = (s32[1,1,128]{2,1,0:T(1,128)S(1)}, s32[1,1,128]{2,1,0:T(1,128)}, u32[]{:S(2)}) copy-start(s32[1,1,128]{2,1,0:T(1,128)} %param.17) | copy-start | bytes 1540
  14.3 20.9 %copy-start.4 = (s32[1,1,32768]{2,1,0:T(1,128)S(1)}, s32[1,1,32768]{2,1,0:T(1,128)}, u32[]{:S(2)}) copy-start(s32[1,1,32768]{2,1,0:T(1,128)} %param.19) | copy-start | bytes 393220
  15.5 48.9 %all-to-all-start = ((bf16[128,8,512]{2,1,0:T(8,128)(2,1)}), bf16[128,8,512]{2,1,0:T(8,128)(2,1)S(1)}, u32[]{:S(2)}, u32[]{:S(2)}) async-start(bf16[128,8,512]{2,1,0:T(8,128)(2,1)} %bitcast_select_fusion), calls=%async_computation | async-start | bytes 2097152 | tf_op jit(solution)/shard_map/all_to_all | solution.py:40
  34.0 220.5 %all-gather.2.cloned.1.call-start = ((), (), s32[]{:S(2)}) async-start(), calls=%async_computation.3 | async-start | bytes 1310720 | tf_op jit(solution)/shard_map/all_gather | solution.py:84
  41.9 3.1 copy-start.7
  46.1 18.3 %copy-start.1 = (bf16[1024,512]{1,0:T(8,128)(2,1)S(1)}, bf16[1024,512]{1,0:T(8,128)(2,1)}, u32[]{:S(2)}) copy-start(bf16[1024,512]{1,0:T(8,128)(2,1)} %param.13) | copy-start | bytes 3145732
  124.7 54.4 %copy-start.5 = (s32[1024]{0:T(1024)S(1)}, s32[1024]{0:T(1024)}, u32[]{:S(2)}) copy-start(s32[1024]{0:T(1024)} %param.20) | copy-start | bytes 12292
  124.7 54.5 %copy-start.2 = (bf16[512,512]{1,0:T(8,128)(2,1)S(1)}, bf16[512,512]{1,0:T(8,128)(2,1)}, u32[]{:S(2)}) copy-start(bf16[512,512]{1,0:T(8,128)(2,1)} %param.14) | copy-start | bytes 1572868
  124.7 47.8 %collective-permute-start = (f32[1024,512]{1,0:T(8,128)S(1)}, f32[1024,512]{1,0:T(8,128)S(1)}, u32[]{:S(2)}, u32[]{:S(2)}) collective-permute-start(f32[1024,512]{1,0:T(8,128)S(1)} %bitcast.82), channel_id=1, source_target_pairs={{0,1},{1,0},{2,3},{3,2},{4,5},{5,4},{6,7},{7,6},{8,9},{9,8},{10,11... | collective-permute-start | bytes 6291464 | tf_op jit(solution)/shard_map/ppermute | solution.py:65
  174.3 48.4 %collective-permute-start.1 = (f32[1024,512]{1,0:T(8,128)}, f32[1024,512]{1,0:T(8,128)S(1)}, u32[]{:S(2)}, u32[]{:S(2)}) collective-permute-start(f32[1024,512]{1,0:T(8,128)} %bitcast_add_fusion), channel_id=1, source_target_pairs={{0,2},{1,3},{2,0},{3,1},{4,6},{5,7},{6,4},{7,5},{8,10},{9,11},{10,... | collective-permute-start | bytes 6291464 | tf_op jit(solution)/shard_map/ppermute | solution.py:65
  223.9 0.7 copy-start.3
  322.1 45.9 %all-to-all-start.1 = ((bf16[128,8,512]{2,1,0:T(8,128)(2,1)}), bf16[128,8,512]{2,1,0:T(8,128)(2,1)}, u32[]{:S(2)}, u32[]{:S(2)}) async-start(bf16[128,8,512]{2,1,0:T(8,128)(2,1)} %bitcast.21), calls=%async_computation.1 | async-start | bytes 2097152 | tf_op jit(solution)/shard_map/all_to_all | solution.py:103
  337.9 146.3 %reduce-scatter.2.cloned.1.call-start = ((), (), s32[]{:S(2)}) async-start(), calls=%async_computation.4 | async-start | bytes 1310720 | tf_op jit(solution)/shard_map/reduce_scatter | solution.py:109
Sparse Core Ops, SparseCore 0:
  228.0 26.4 all-gather.1
  377.3 20.4 reduce-scatter.1
